TPU v7x, 32 devices: a whole 2x2x4 slice. The times are simulated.
32 devices in a mesh: mem: 8 (over z, y), lev: 4 (over x, core).
Axes of the slice: x: 2, y: 2, z: 4, core: 2. Of those that a mesh axis runs over, the one named last changes fastest.
Arguments:
- prior_ensemble_stack: float32 [16, 20, 64, 512], P('mem', 'lev'), may hold values from -6 to 6
- vertical_cfl_ratio: float32 [20, 64, 512], P('lev'), may hold values from -0.35 to 0.35
- horizontal_cfl_ratio: float32 [20, 64, 512], P('lev'), may hold values from -0.35 to 0.35
- spreading_coefficient: float32 [20], P('lev'), may hold values from 0.02 to 0.2
- obs_cells: int32 [2, 16], replicated, may hold values from 0 to 32767
- obs_slabs: int32 [2, 16], replicated, may hold values from 0 to 19
- obs_values: float32 [2, 16], replicated, may hold values from -6 to 6
- obs_error: float32 [2, 16], replicated, may hold values from 0.25 to 2
Outputs:
- analysis: float32 [16, 20, 64, 512], P('mem', 'lev')
All inputs are finite; a program needn't handle non-finite values.
Results may differ from a plain program's by a relative error of at most 0.0001.
Values sent between devices are 32-bit elements; how exact they have to be, the bound alone decides.
No kernel may reach another device: no remote copies, remote signals or barrier semaphores. Data moves between devices by JAX's collectives and lax.ppermute only.
A program may use at most 256 MiB of HBM per device.

v0:
```python
import jax
import jax.numpy as jnp
from jax import lax
from jax.sharding import PartitionSpec as P

NX = 512
STEPS = 2
LOC_HALF = 64


def predicted_model_vector(
    ensemble_gridded_values, vertical_cfl_ratio, horizontal_cfl_ratio, spreading_coefficient
):
    diffuse = spreading_coefficient[:, None, None]
    for time_step in range(STEPS):
        widths = [(0, 0)] * (ensemble_gridded_values.ndim - 2) + [(1, 1), (1, 1)]
        padded = jnp.pad(ensemble_gridded_values, widths, mode="edge")
        east_cell = padded[..., 1:-1, 2:]
        west_cell = padded[..., 1:-1, :-2]
        north_cell = padded[..., 2:, 1:-1]
        south_cell = padded[..., :-2, 1:-1]
        ensemble_gridded_values = (
            ensemble_gridded_values
            - 0.5 * vertical_cfl_ratio * (east_cell - west_cell)
            - 0.5 * horizontal_cfl_ratio * (north_cell - south_cell)
            + diffuse
            * (east_cell + west_cell + north_cell + south_cell - 4.0 * ensemble_gridded_values)
        )
    return ensemble_gridded_values


def grid_distance(cells_a, cells_b):
    row_gap = (cells_a[:, None] // NX - cells_b[None, :] // NX).astype(jnp.float32)
    col_gap = (cells_a[:, None] % NX - cells_b[None, :] % NX).astype(jnp.float32)
    return jnp.sqrt(row_gap * row_gap + col_gap * col_gap)


def gaspari_taper(dist):
    scaled = dist / LOC_HALF
    inner_portion = (
        ((-0.25 * scaled + 0.5) * scaled + 0.625) * scaled - 5.0 / 3.0
    ) * scaled * scaled + 1.0
    safe_ratio = jnp.maximum(scaled, 1.0)
    outer_portion = (
        ((((scaled / 12.0 - 0.5) * scaled + 0.625) * scaled + 5.0 / 3.0) * scaled - 5.0) * scaled
        + 4.0
        - 2.0 / (3.0 * safe_ratio)
    )
    return jnp.where(scaled <= 1.0, inner_portion, jnp.where(scaled < 2.0, outer_portion, 0.0))


def obs_space(prior_rows, row_cells, first_row, obs_cell, obs_value, obs_var):
    member_count = prior_rows.shape[1]
    reach_table = gaspari_taper(grid_distance(row_cells, obs_cell))

    def advance_obs(current, position):
        own_row = lax.dynamic_index_in_dim(current, first_row + position, 0, False)
        row_mean = jnp.mean(own_row)
        anomaly = own_row - row_mean
        spread = jnp.sum(anomaly * anomaly) / (member_count - 1) + 1e-06
        error_var = lax.dynamic_index_in_dim(obs_var, position, 0, False)
        seen_value = lax.dynamic_index_in_dim(obs_value, position, 0, False)
        shrink = jnp.sqrt(error_var / (spread + error_var))
        increment = (
            (row_mean * error_var + seen_value * spread) / (spread + error_var)
            - row_mean
            + (shrink - 1.0) * anomaly
        )
        centered = current - jnp.mean(current, axis=1, keepdims=True)
        slopes = jnp.dot(centered, anomaly, precision=lax.Precision.HIGHEST) / (
            (member_count - 1) * spread
        )
        weight = lax.dynamic_index_in_dim(reach_table, position, 1, False)
        current = current + (weight * slopes)[:, None] * increment[None, :]
        return (current, (anomaly, spread, increment))

    positions = jnp.arange(obs_cell.shape[0], dtype=jnp.int32)
    prior_rows, obs_plan = lax.scan(advance_obs, prior_rows, positions)
    return (obs_plan, prior_rows)


def settle(state_rows, obs_plan, cell_loc):
    prior_anoms, spreads, increments = obs_plan
    member_count = state_rows.shape[0]
    centered = state_rows - jnp.mean(state_rows, axis=0, keepdims=True)
    cross_cov = jnp.einsum(
        "km,msc->ksc", prior_anoms, centered, precision=lax.Precision.HIGHEST
    ) / (member_count - 1)
    incr_anom = increments - jnp.mean(increments, axis=1, keepdims=True)
    incr_link = jnp.dot(incr_anom, prior_anoms.T, precision=lax.Precision.HIGHEST) / (
        member_count - 1
    )

    def solve_step(weights, position):
        column = lax.dynamic_index_in_dim(incr_link, position, 1, False)
        summed_total = lax.dynamic_index_in_dim(cross_cov, position, 0, False) + jnp.einsum(
            "j,jsc->sc", column, weights, precision=lax.Precision.HIGHEST
        )
        taper_row = lax.dynamic_index_in_dim(cell_loc, position, 0, False)
        update_row = (
            taper_row[None, :]
            * summed_total
            / lax.dynamic_index_in_dim(spreads, position, 0, False)
        )
        return (lax.dynamic_update_index_in_dim(weights, update_row, position, 0), None)

    positions = jnp.arange(cross_cov.shape[0], dtype=jnp.int32)
    weights, unused = lax.scan(solve_step, jnp.zeros_like(cross_cov), positions)
    return state_rows + jnp.einsum(
        "km,ksc->msc", increments, weights, precision=lax.Precision.HIGHEST
    )


def pick_rows(state_rows, obs_slab, obs_cell, slab_base, cell_base):
    slab_dev = state_rows.shape[1]
    cell_dev = state_rows.shape[2]
    slab_off = obs_slab - slab_base
    cell_off = obs_cell - cell_base
    inside = (slab_off >= 0) & (slab_off < slab_dev) & (cell_off >= 0) & (cell_off < cell_dev)
    taken_rows = state_rows[
        :, jnp.clip(slab_off, 0, slab_dev - 1), jnp.clip(cell_off, 0, cell_dev - 1)
    ]
    return jnp.where(inside[:, None], taken_rows.T, 0.0)


def body(
    prior_ensemble_stack,
    vertical_cfl_ratio,
    horizontal_cfl_ratio,
    spreading_coefficient,
    obs_cells,
    obs_slabs,
    obs_values,
    obs_error,
):
    mem_dev, slab_dev, grid_rows, grid_cols = prior_ensemble_stack.shape
    cell_total = grid_rows * grid_cols
    cell_dev = cell_total // lax.axis_size("mem")
    batch_count = obs_cells.shape[0]
    ensemble_gridded_values = predicted_model_vector(
        prior_ensemble_stack, vertical_cfl_ratio, horizontal_cfl_ratio, spreading_coefficient
    )
    by_cells = ensemble_gridded_values.reshape(mem_dev, slab_dev, cell_total)
    cell_base = lax.axis_index("mem") * cell_dev
    slab_base = lax.axis_index("lev") * slab_dev
    local_cells = cell_base + jnp.arange(cell_dev, dtype=jnp.int32)
    cell_locs = [
        gaspari_taper(grid_distance(obs_cells[batch_no], local_cells))
        for batch_no in range(batch_count)
    ]
    state_rows = lax.all_to_all(by_cells, "mem", split_axis=2, concat_axis=0, tiled=True)
    for batch_no in range(batch_count):
        partial_value = pick_rows(
            state_rows, obs_slabs[batch_no], obs_cells[batch_no], slab_base, cell_base
        )
        prior_rows = lax.psum(partial_value, ("mem", "lev"))
        obs_plan, carried = obs_space(
            prior_rows,
            obs_cells[batch_no],
            0,
            obs_cells[batch_no],
            obs_values[batch_no],
            obs_error[batch_no],
        )
        state_rows = settle(state_rows, obs_plan, cell_locs[batch_no])
    result = lax.all_to_all(state_rows, "mem", split_axis=0, concat_axis=2, tiled=True)
    return result.reshape(prior_ensemble_stack.shape)


def solution(mesh):
    in_specs = (
        P("mem", "lev", None, None),
        P("lev", None, None),
        P("lev", None, None),
        P("lev"),
        P(),
        P(),
        P(),
        P(),
    )
    out_specs = P("mem", "lev", None, None)
    return jax.shard_map(body, mesh=mesh, in_specs=in_specs, out_specs=out_specs, check_vma=False)
```

profile of v0, /device:TPU:0, one launch (start us, length us, event | category | flops | bytes accessed | tf_op | source)
XLA Modules:
  0.0 932.9 jit_solution(16619717677496745712)
XLA Ops:
  1.1 1.5 broadcast_multiply_fusion.2
  2.7 2.2 multiply_add_fusion.5
  5.0 2.2 multiply_add_fusion.4
  7.2 22.3 %copy.76 = f32[2,5,64,512]{1,0,3,2:T(2,128)} copy(f32[2,5,64,512]{3,2,1,0:T(8,128)S(1)} %multiply_add_fusion.4) | data formatting | bytes 2621440 | tf_op jit(solution)/shard_map/reshape | solution.py:143
  29.5 53.2 %reshape.447 = f32[8,1,40960]{2,1,0:T(1,128)} reshape(f32[32768,2,5]{2,1,0:T(2,128)} %bitcast.261) | data formatting | bytes 2621440
  82.7 7.6 all-to-all-start
  92.0 1.6 fusion.55
  93.6 27.9 %all-to-all-done = f32[8,1,40960]{2,1,0:T(1,128)S(1)} async-done(((f32[8,1,40960]{2,1,0:T(1,128)}), f32[8,1,40960]{2,1,0:T(1,128)S(1)}, u32[]{:S(2)}, u32[]{:S(2)}) %all-to-all-start) | async-done | bytes 1310752 | tf_op jit(solution)/shard_map/all_to_all | solution.py:151
  122.0 3.8 reduce.3
  125.8 62.1 %reshape.448 = f32[32768,2,5]{2,1,0:T(2,128)} reshape(f32[8,40960]{1,0:T(8,128)S(1)} %reduce.3) | data formatting | bytes 2621440
  187.9 26.8 %copy.73 = f32[2,5,8,4096]{3,2,0,1:T(8,128)S(1)} copy(f32[2,5,8,4096]{1,0,3,2:T(2,128)} %bitcast.262) | data formatting | bytes 2621440 | tf_op jit(solution)/shard_map/all_to_all | solution.py:151
  216.8 5.5 copy.51
  222.4 1.5 gather_fusion
  223.9 37.7 %psum.14 = f32[16,16]{1,0:T(8,128)S(1)} all-reduce(f32[16,16]{1,0:T(8,128)S(1)} %broadcast_select_fusion.1), channel_id=1, replica_groups=mesh['mem'=8,'lev'=4] {'mem','lev'}, use_global_device_ids=true, to_apply=%region_0.1 | all-reduce | flops 256 | bytes 2048 | tf_op jit(solution)/shard_map/psum | solution.py:156
  261.6 153.8 %while.56 = (s32[]{:T(128)}, f32[16,16]{1,0:T(8,128)S(1)}, f32[16,16]{1,0:T(8,128)S(1)}, f32[16]{0:T(128)S(1)}, f32[16,16]{1,0:T(8,128)S(1)}, /*index=5*/s32[16]...) while((s32[]{:T(128)}, f32[16,16]{1,0:T(8,128)S(1)}, ...), condition=%wide.region_5.6_spmd, body=%wide.region_1.5_spmd.sunk | while | flops 4271 | bytes 5831 | solution.py:78
  415.9 2.2 convolution_multiply_fusion.1
  418.3 118.7 %while.57 = (s32[]{:T(128)}, f32[16,5,4096]{2,1,0:T(8,128)S(1)}, s32[16]{0:T(128)S(1)}, f32[16,4096]{1,0:T(8,128)}, f32[16,5,4096]{2,0,1:T(8,128)}, /*index=5*/f...) while((s32[]{:T(128)}, f32[16,5,4096]{2,1,0:T(8,128)S(1)}, s32[16]{0:T(128)S(1)}, ...), condition=%wide.region_9.10_spmd, body=%wide.region_8.9_spmd.sunk | while | flops 3993605 | bytes 2687667 | solution.py:108
  420.9 1.4 fusion.130
  428.3 1.4 fusion.130
  429.7 1.2 constant_dynamic-slice_fusion.12
  435.7 1.4 fusion.130
  443.1 1.4 fusion.130
  450.5 1.4 fusion.130
  458.0 1.4 fusion.130
  465.4 1.4 fusion.130
  472.8 1.4 fusion.130
  480.2 1.4 fusion.130
  481.7 1.2 constant_dynamic-slice_fusion.12
  487.6 1.4 fusion.130
  489.1 1.2 constant_dynamic-slice_fusion.12
  495.1 1.4 fusion.130
  496.5 1.2 constant_dynamic-slice_fusion.12
  502.5 1.4 fusion.130
  503.9 1.2 constant_dynamic-slice_fusion.12
  509.9 1.4 fusion.130
  517.3 1.4 fusion.130
  524.7 1.4 fusion.130
  532.1 1.4 fusion.130
  537.0 3.3 fusion.97
  540.4 5.5 copy.57
  545.8 1.5 gather_fusion.1
  547.4 41.9 %psum.15 = f32[16,16]{1,0:T(8,128)S(1)} all-reduce(f32[16,16]{1,0:T(8,128)S(1)} %broadcast_select_fusion), channel_id=1, replica_groups=mesh['mem'=8,'lev'=4] {'mem','lev'}, use_global_device_ids=true, to_apply=%region_10.11 | all-reduce | flops 256 | bytes 2048 | tf_op jit(solution)/shard_map/psum | solution.py:156
  589.3 163.1 %while.58 = (s32[]{:T(128)}, f32[16,16]{1,0:T(8,128)S(1)}, f32[16,16]{1,0:T(8,128)S(1)}, f32[16]{0:T(128)S(1)}, f32[16,16]{1,0:T(8,128)S(1)}, /*index=5*/s32[16]...) while((s32[]{:T(128)}, f32[16,16]{1,0:T(8,128)S(1)}, ...), condition=%wide.region_15.16_spmd, body=%wide.region_11.15_spmd.sunk | while | flops 4271 | bytes 5831 | solution.py:78
  753.0 2.2 convolution_multiply_fusion
  755.9 120.0 %while.59 = (s32[]{:T(128)}, f32[16,5,4096]{2,1,0:T(8,128)S(1)}, s32[16]{0:T(128)S(1)}, f32[16,4096]{1,0:T(8,128)}, f32[16,5,4096]{2,0,1:T(8,128)}, /*index=5*/f...) while((s32[]{:T(128)}, f32[16,5,4096]{2,1,0:T(8,128)S(1)}, s32[16]{0:T(128)S(1)}, ...), condition=%wide.region_19.20_spmd, body=%wide.region_18.19_spmd.sunk | while | flops 3993605 | bytes 2687667 | solution.py:108
  758.5 1.4 fusion.140
  766.0 1.4 fusion.140
  773.5 1.4 fusion.140
  781.0 1.4 fusion.140
  788.5 1.4 fusion.140
  796.0 1.4 fusion.140
  803.5 1.4 fusion.140
  811.0 1.4 fusion.140
  818.5 1.4 fusion.140
  826.0 1.4 fusion.140
  833.5 1.4 fusion.140
  841.0 1.4 fusion.140
  848.5 1.4 fusion.140
  856.0 1.4 fusion.140
  863.5 1.4 fusion.140
  871.0 1.4 fusion.140
  875.9 1.9 convolution_add_fusion
  878.6 51.7 %all_to_all.33 = f32[16,5,4096]{2,1,0:T(8,128)S(1)} all-to-all(f32[16,5,4096]{2,1,0:T(8,128)S(1)} %copy.63), channel_id=1, replica_groups=mesh['mem'=8,'lev'=4] {'mem'}, dimensions={0} | all-to-all | bytes 2621440 | tf_op jit(solution)/shard_map/all_to_all | solution.py:166
  931.1 1.3 reshape.421
  (637 shorter events, 262.4 us)
Async XLA Ops:
  1.0 1.7 copy-start.1
  1.0 1.7 copy-start.4
  82.7 7.7 copy-start.2
  82.7 8.7 copy-start.3
  82.7 8.8 copy-start.5
  82.7 8.8 copy-start.6
  82.7 38.8 %all-to-all-start = ((f32[8,1,40960]{2,1,0:T(1,128)}), f32[8,1,40960]{2,1,0:T(1,128)S(1)}, u32[]{:S(2)}, u32[]{:S(2)}) async-start(f32[8,1,40960]{2,1,0:T(1,128)} %reshape.447), calls=%async_computation | async-start | bytes 2621440 | tf_op jit(solution)/shard_map/all_to_all | solution.py:151
  216.8 199.1 %copy-start = (f32[16,5,4096]{2,0,1:T(8,128)}, f32[16,5,4096]{2,0,1:T(8,128)S(1)}, u32[]{:S(2)}) copy-start(f32[16,5,4096]{2,0,1:T(8,128)S(1)} %all_to_all.27) | copy-start | bytes 3932164
  540.3 49.0 %copy-start.7 = (f32[16]{0:T(128)S(1)}, f32[16]{0:T(128)}, u32[]{:S(2)}) copy-start(f32[16]{0:T(128)} %get-tuple-element.825) | copy-start | bytes 196
  540.4 49.0 %copy-start.8 = (f32[16]{0:T(128)S(1)}, f32[16]{0:T(128)}, u32[]{:S(2)}) copy-start(f32[16]{0:T(128)} %get-tuple-element.824) | copy-start | bytes 196
  752.4 0.6 copy-start.9
  755.3 0.7 copy-start.10
where the time goes:
time: 946 us; the launch traced here: 933 us
  local copies, waits for them, and re-layouts  358 us (38%)
  loops' own time  250 us (26%)
  blocking collectives  131 us (14%)
  other arithmetic  83.4 us (9%)
  matrix products  73.5 us (8%)
  waiting for transfers between devices  27.9 us (3%)
    another operation x2, loops' own time, obs_space(): prior_rows, obs_plan = lax.scan(advance_obs, prior_rows, positions)  189 us
    unnamed x24, local copies, waits for them, and re-layouts  116 us
    psum x2, blocking collectives, body(): prior_rows = lax.psum(partial_value, ('mem', 'lev'))  79.6 us
    another operation x2, loops' own time, settle(): weights, unused = lax.scan(solve_step, jnp.zeros_like(cross_cov), positions)  61.9 us
    all_to_all x1, blocking collectives, body(): lax.all_to_all(state_rows, 'mem', split_axis=0, concat_axis=2, tiled=True)  51.7 us
    dot_general x32, matrix products, solve_step(): jnp.einsum('j,jsc->sc', column, weights, precision=lax.Precision.HIGHEST)  46.1 us
    dynamic_slice x64, local copies, waits for them, and re-layouts, obs_space(): prior_rows, obs_plan = lax.scan(advance_obs, prior_rows, positions)  40.3 us
    dynamic_slice x32, local copies, waits for them, and re-layouts, solve_step(): lax.dynamic_index_in_dim(cross_cov, position, 0, False)  36.9 us
  transfers between devices with their start and end apart: 1, of which 1 were waited for; matrix products, arithmetic and copies ran while one was open for 0% of the time, Pallas kernels for 0%

commit v1 on v0

--- a/solution.py
+++ b/solution.py
@@ -6,6 +6,18 @@
 NX = 512
 STEPS = 2
 LOC_HALF = 64
+
+
+def cut_along(shard, dim, size):
+    lengths = shard.shape
+    parts = shard.reshape(*lengths[:dim], size, lengths[dim] // size, *lengths[dim + 1 :])
+    return jnp.moveaxis(parts, dim, 0)
+
+
+def in_order(pieces, dim):
+    pieces = jnp.moveaxis(pieces, 0, dim)
+    shape = pieces.shape
+    return pieces.reshape(*shape[:dim], shape[dim] * shape[dim + 1], *shape[dim + 2 :])
 
 
 def predicted_model_vector(
@@ -148,7 +160,14 @@
         gaspari_taper(grid_distance(obs_cells[batch_no], local_cells))
         for batch_no in range(batch_count)
     ]
-    state_rows = lax.all_to_all(by_cells, "mem", split_axis=2, concat_axis=0, tiled=True)
+    devices, index = (lax.axis_size("mem"), lax.axis_index("mem"))
+    blocks = cut_along(by_cells, 2, devices)
+    finished = [blocks[index]]
+    for hop in range(1, devices):
+        sent = blocks[index ^ hop]
+        finished.append(lax.ppermute(sent, "mem", [(i, i ^ hop) for i in range(devices)]))
+    blocks = jnp.stack(finished)[index ^ jnp.arange(devices)]
+    state_rows = in_order(blocks, 0)
     for batch_no in range(batch_count):
         partial_value = pick_rows(
             state_rows, obs_slabs[batch_no], obs_cells[batch_no], slab_base, cell_base

time: 946 us -> 768 us (0.81)
  local copies, waits for them, and re-layouts: 358 us -> 199 us
  waiting for transfers between devices: 27.9 us -> 14.4 us
    unnamed x24 -> x36, local copies, waits for them, and re-layouts: 116 us -> 2 us
    all_to_all x5 -> x0, local copies, waits for them, and re-layouts: 34.7 us -> none  [body(): lax.all_to_all(by_cells, 'mem', split_axis=2, concat_axis=0, tiled=True)]
    all_to_all x1 -> x0, waiting for transfers between devices: 27.9 us -> none  [body(): lax.all_to_all(by_cells, 'mem', split_axis=2, concat_axis=0, tiled=True)]
    reshape x1 -> x2, local copies, waits for them, and re-layouts: 22.3 us -> 7.66 us  [in_order(): pieces.reshape(*shape[:dim], shape[dim] * shape[dim + 1], *shape[dim + 2:])]
    ppermute x0 -> x7, waiting for transfers between devices: none -> 14.4 us  [body(): lax.ppermute(sent, 'mem', [(i, i ^ hop) for i in range(devices)])]
    ppermute x0 -> x7, starting transfers between devices: none -> 12.9 us  [body(): lax.ppermute(sent, 'mem', [(i, i ^ hop) for i in range(devices)])]
  transfers between devices with their start and end apart: 1 -> 7, of which waited for: 1 -> 2; matrix products, arithmetic and copies ran while one was open for 0% -> 1% of each run, Pallas kernels for 0% -> 0%
where the time goes in v1:
time: 768 us; the launch traced here: 761 us
  loops' own time  246 us (32%)
  local copies, waits for them, and re-layouts  199 us (26%)
  blocking collectives  137 us (18%)
  other arithmetic  78.5 us (10%)
  matrix products  73.5 us (10%)
  waiting for transfers between devices  14.4 us (2%)
  starting transfers between devices  12.9 us (2%)
    another operation x2, loops' own time, obs_space(): prior_rows, obs_plan = lax.scan(advance_obs, prior_rows, positions)  187 us
    psum x2, blocking collectives, body(): prior_rows = lax.psum(partial_value, ('mem', 'lev'))  84.8 us
    another operation x2, loops' own time, settle(): weights, unused = lax.scan(solve_step, jnp.zeros_like(cross_cov), positions)  58.6 us
    all_to_all x1, blocking collectives, body(): lax.all_to_all(state_rows, 'mem', split_axis=0, concat_axis=2, tiled=True)  52.3 us
    dot_general x32, matrix products, solve_step(): jnp.einsum('j,jsc->sc', column, weights, precision=lax.Precision.HIGHEST)  46.1 us
    dynamic_slice x64, local copies, waits for them, and re-layouts, obs_space(): prior_rows, obs_plan = lax.scan(advance_obs, prior_rows, positions)  39.4 us
    dynamic_slice x32, local copies, waits for them, and re-layouts, solve_step(): lax.dynamic_index_in_dim(cross_cov, position, 0, False)  36.9 us
    dynamic_slice x32, local copies, waits for them, and re-layouts, solve_step(): taper_row = lax.dynamic_index_in_dim(cell_loc, position, 0, False)  29.6 us
  transfers between devices with their start and end apart: 7, of which 2 were waited for; matrix products, arithmetic and copies ran while one was open for 1% of the time, Pallas kernels for 0%

profile of v1, /device:TPU:0, one launch (start us, length us, event | category | flops | bytes accessed | tf_op | source)
XLA Modules:
  0.0 761.0 jit_solution(3414355131393233158)
XLA Ops:
  1.1 1.5 broadcast_multiply_fusion.2
  2.7 2.2 multiply_add_fusion.5
  5.0 2.2 multiply_add_fusion.4
  7.4 1.3 constant_dynamic-slice_fusion.8
  8.9 3.1 collective-permute-start
  12.1 1.6 collective-permute-start.1
  14.1 3.0 collective-permute-start.3
  17.3 1.4 collective-permute-start.4
  19.6 1.6 fusion.55
  22.3 3.7 collective-permute-start.5
  26.4 14.1 %collective-permute-done.4 = f32[2,5,4096]{2,0,1:T(2,128)S(1)} collective-permute-done((f32[2,5,4096]{2,0,1:T(2,128)S(1)}, f32[2,5,4096]{2,0,1:T(2,128)S(1)}, u32[]{:S(2)}, u32[]{:S(2)}) %collective-permute-start.4) | collective-permute-done | bytes 163872 | tf_op jit(solution)/shard_map/ppermute | solution.py:168
  40.7 1.9 gather_fusion
  43.8 2.2 reshape.451
  46.0 5.5 copy.45
  51.5 1.5 gather_fusion.1
  53.0 45.2 %psum.14 = f32[16,16]{1,0:T(8,128)S(1)} all-reduce(f32[16,16]{1,0:T(8,128)S(1)} %broadcast_select_fusion.1), channel_id=1, replica_groups=mesh['mem'=8,'lev'=4] {'mem','lev'}, use_global_device_ids=true, to_apply=%region_0.1 | all-reduce | flops 256 | bytes 2048 | tf_op jit(solution)/shard_map/psum | solution.py:175
  98.3 152.7 %while.56 = (s32[]{:T(128)}, f32[16,16]{1,0:T(8,128)S(1)}, f32[16,16]{1,0:T(8,128)S(1)}, f32[16]{0:T(128)S(1)}, f32[16,16]{1,0:T(8,128)S(1)}, /*index=5*/s32[16]...) while((s32[]{:T(128)}, f32[16,16]{1,0:T(8,128)S(1)}, ...), condition=%wide.region_5.6_spmd, body=%wide.region_1.5_spmd.sunk | while | flops 4271 | bytes 5831 | solution.py:90
  252.0 2.2 convolution_multiply_fusion.1
  254.4 114.3 %while.57 = (s32[]{:T(128)}, f32[16,5,4096]{2,1,0:T(8,128)S(1)}, s32[16]{0:T(128)S(1)}, f32[16,4096]{1,0:T(8,128)}, f32[16,5,4096]{2,0,1:T(8,128)}, /*index=5*/f...) while((s32[]{:T(128)}, f32[16,5,4096]{2,1,0:T(8,128)S(1)}, s32[16]{0:T(128)S(1)}, ...), condition=%wide.region_9.10_spmd, body=%wide.region_8.9_spmd.sunk | while | flops 3993605 | bytes 2687667 | solution.py:120
  256.8 1.4 fusion.132
  263.9 1.4 fusion.132
  265.4 1.2 constant_dynamic-slice_fusion.20
  271.1 1.4 fusion.132
  278.2 1.4 fusion.132
  279.7 1.2 constant_dynamic-slice_fusion.20
  285.4 1.4 fusion.132
  286.8 1.2 constant_dynamic-slice_fusion.20
  292.5 1.4 fusion.132
  299.6 1.4 fusion.132
  306.8 1.4 fusion.132
  313.9 1.4 fusion.132
  321.1 1.4 fusion.132
  328.2 1.4 fusion.132
  335.4 1.4 fusion.132
  342.5 1.4 fusion.132
  349.6 1.4 fusion.132
  356.8 1.4 fusion.132
  363.9 1.4 fusion.132
  368.7 3.3 fusion.99
  372.1 5.5 copy.51
  377.5 1.5 gather_fusion.2
  379.1 39.6 %psum.15 = f32[16,16]{1,0:T(8,128)S(1)} all-reduce(f32[16,16]{1,0:T(8,128)S(1)} %broadcast_select_fusion), channel_id=1, replica_groups=mesh['mem'=8,'lev'=4] {'mem','lev'}, use_global_device_ids=true, to_apply=%region_10.11 | all-reduce | flops 256 | bytes 2048 | tf_op jit(solution)/shard_map/psum | solution.py:175
  418.7 163.1 %while.58 = (s32[]{:T(128)}, f32[16,16]{1,0:T(8,128)S(1)}, f32[16,16]{1,0:T(8,128)S(1)}, f32[16]{0:T(128)S(1)}, f32[16,16]{1,0:T(8,128)S(1)}, /*index=5*/s32[16]...) while((s32[]{:T(128)}, f32[16,16]{1,0:T(8,128)S(1)}, ...), condition=%wide.region_15.16_spmd, body=%wide.region_11.15_spmd.sunk | while | flops 4271 | bytes 5831 | solution.py:90
  582.4 2.2 convolution_multiply_fusion
  585.3 118.7 %while.59 = (s32[]{:T(128)}, f32[16,5,4096]{2,1,0:T(8,128)S(1)}, s32[16]{0:T(128)S(1)}, f32[16,4096]{1,0:T(8,128)}, f32[16,5,4096]{2,0,1:T(8,128)}, /*index=5*/f...) while((s32[]{:T(128)}, f32[16,5,4096]{2,1,0:T(8,128)S(1)}, s32[16]{0:T(128)S(1)}, ...), condition=%wide.region_19.20_spmd, body=%wide.region_18.19_spmd.sunk | while | flops 3993605 | bytes 2687667 | solution.py:120
  587.8 1.4 fusion.142
  595.2 1.4 fusion.142
  602.6 1.4 fusion.142
  610.1 1.4 fusion.142
  617.5 1.4 fusion.142
  624.9 1.4 fusion.142
  632.3 1.4 fusion.142
  639.8 1.4 fusion.142
  647.2 1.4 fusion.142
  654.6 1.4 fusion.142
  662.0 1.4 fusion.142
  669.4 1.4 fusion.142
  676.9 1.4 fusion.142
  684.3 1.4 fusion.142
  691.7 1.4 fusion.142
  699.1 1.4 fusion.142
  704.0 1.9 convolution_add_fusion
  706.7 52.3 %all_to_all.15 = f32[16,5,4096]{2,1,0:T(8,128)S(1)} all-to-all(f32[16,5,4096]{2,1,0:T(8,128)S(1)} %copy.57), channel_id=1, replica_groups=mesh['mem'=8,'lev'=4] {'mem'}, dimensions={0} | all-to-all | bytes 2621440 | tf_op jit(solution)/shard_map/all_to_all | solution.py:185
  759.8 1.3 reshape.452
  (663 shorter events, 263.6 us)
Async XLA Ops:
  1.0 1.7 copy-start.1
  1.0 1.7 copy-start.4
  8.7 9.9 %copy-start.2 = (s32[2,16]{1,0:T(2,128)S(1)}, s32[2,16]{1,0:T(2,128)}, u32[]{:S(2)}) copy-start(s32[2,16]{1,0:T(2,128)} %param.20) | copy-start | bytes 388
  8.8 9.9 %copy-start.3 = (s32[2,16]{1,0:T(2,128)S(1)}, s32[2,16]{1,0:T(2,128)}, u32[]{:S(2)}) copy-start(s32[2,16]{1,0:T(2,128)} %param.21) | copy-start | bytes 388
  8.8 10.1 %copy-start.5 = (f32[2,16]{1,0:T(2,128)S(1)}, f32[2,16]{1,0:T(2,128)}, u32[]{:S(2)}) copy-start(f32[2,16]{1,0:T(2,128)} %param.22) | copy-start | bytes 388
  8.8 10.1 %copy-start.6 = (f32[2,16]{1,0:T(2,128)S(1)}, f32[2,16]{1,0:T(2,128)}, u32[]{:S(2)}) copy-start(f32[2,16]{1,0:T(2,128)} %param.23) | copy-start | bytes 388
  8.9 13.4 %collective-permute-start = (f32[2,5,4096]{2,0,1:T(2,128)S(1)}, f32[2,5,4096]{2,0,1:T(2,128)S(1)}, u32[]{:S(2)}, u32[]{:S(2)}) collective-permute-start(f32[2,5,4096]{2,0,1:T(2,128)S(1)} %bitcast.305), channel_id=1, source_target_pairs={{0,4},{4,0},{8,12},{12,8},{16,20},{20,16},{24,28},{28,24},{1,5},{5... | collective-permute-start | bytes 491528 | tf_op jit(solution)/shard_map/ppermute | solution.py:168
  12.1 13.9 %collective-permute-start.1 = (f32[2,5,4096]{2,0,1:T(2,128)S(1)}, f32[2,5,4096]{2,0,1:T(2,128)S(1)}, u32[]{:S(2)}, u32[]{:S(2)}) collective-permute-start(f32[2,5,4096]{2,0,1:T(2,128)S(1)} %bitcast.304), channel_id=1, source_target_pairs={{0,8},{4,12},{8,0},{12,4},{16,24},{20,28},{24,16},{28,20},{1,9},{5... | collective-permute-start | bytes 491528 | tf_op jit(solution)/shard_map/ppermute | solution.py:168
  13.9 12.5 %collective-permute-start.2 = (f32[2,5,4096]{2,0,1:T(2,128)S(1)}, f32[2,5,4096]{2,0,1:T(2,128)S(1)}, u32[]{:S(2)}, u32[]{:S(2)}) collective-permute-start(f32[2,5,4096]{2,0,1:T(2,128)S(1)} %bitcast.303), channel_id=1, source_target_pairs={{0,12},{4,8},{8,4},{12,0},{16,28},{20,24},{24,20},{28,16},{1,13},{... | collective-permute-start | bytes 491528 | tf_op jit(solution)/shard_map/ppermute | solution.py:168
  14.1 12.3 %collective-permute-start.3 = (f32[2,5,4096]{2,0,1:T(2,128)S(1)}, f32[2,5,4096]{2,0,1:T(2,128)S(1)}, u32[]{:S(2)}, u32[]{:S(2)}) collective-permute-start(f32[2,5,4096]{2,0,1:T(2,128)S(1)} %bitcast.302), channel_id=1, source_target_pairs={{0,16},{4,20},{8,24},{12,28},{16,0},{20,4},{24,8},{28,12},{1,17},{... | collective-permute-start | bytes 491528 | tf_op jit(solution)/shard_map/ppermute | solution.py:168
  17.3 23.3 %collective-permute-start.4 = (f32[2,5,4096]{2,0,1:T(2,128)S(1)}, f32[2,5,4096]{2,0,1:T(2,128)S(1)}, u32[]{:S(2)}, u32[]{:S(2)}) collective-permute-start(f32[2,5,4096]{2,0,1:T(2,128)S(1)} %bitcast.301), channel_id=1, source_target_pairs={{0,20},{4,16},{8,28},{12,24},{16,4},{20,0},{24,12},{28,8},{1,21},{... | collective-permute-start | bytes 491528 | tf_op jit(solution)/shard_map/ppermute | solution.py:168
  22.3 18.3 %collective-permute-start.5 = (f32[2,5,4096]{2,0,1:T(2,128)S(1)}, f32[2,5,4096]{2,0,1:T(2,128)S(1)}, u32[]{:S(2)}, u32[]{:S(2)}) collective-permute-start(f32[2,5,4096]{2,0,1:T(2,128)S(1)} %bitcast.307), channel_id=1, source_target_pairs={{0,24},{4,28},{8,16},{12,20},{16,8},{20,12},{24,0},{28,4},{1,25},{... | collective-permute-start | bytes 491528 | tf_op jit(solution)/shard_map/ppermute | solution.py:168
  26.0 14.6 %collective-permute-start.6 = (f32[2,5,4096]{2,0,1:T(2,128)S(1)}, f32[2,5,4096]{2,0,1:T(2,128)S(1)}, u32[]{:S(2)}, u32[]{:S(2)}) collective-permute-start(f32[2,5,4096]{2,0,1:T(2,128)S(1)} %bitcast.306), channel_id=1, source_target_pairs={{0,28},{4,24},{8,20},{12,16},{16,12},{20,8},{24,4},{28,0},{1,29},{... | collective-permute-start | bytes 491528 | tf_op jit(solution)/shard_map/ppermute | solution.py:168
  46.0 206.0 %copy-start = (f32[16,5,4096]{2,0,1:T(8,128)}, f32[16,5,4096]{2,0,1:T(8,128)S(1)}, u32[]{:S(2)}) copy-start(f32[16,5,4096]{2,0,1:T(8,128)S(1)} %reshape.451) | copy-start | bytes 3932164
  372.1 46.7 %copy-start.7 = (f32[16]{0:T(128)S(1)}, f32[16]{0:T(128)}, u32[]{:S(2)}) copy-start(f32[16]{0:T(128)} %get-tuple-element.801) | copy-start | bytes 196
  372.1 46.7 %copy-start.8 = (f32[16]{0:T(128)S(1)}, f32[16]{0:T(128)}, u32[]{:S(2)}) copy-start(f32[16]{0:T(128)} %get-tuple-element.800) | copy-start | bytes 196
  581.8 0.6 copy-start.9
  584.7 0.7 copy-start.10
